TPU v7x, 256 devices: a whole 4x4x8 slice. The times are simulated.
256 devices in a mesh: batch: 2 (over y_lo), tm: 64 (over z, x, y_hi), mp: 2 (over core).
Axes of the slice: x: 4, y: 4 (y_hi: 2, y_lo: 2; y = y_hi * 2 + y_lo), z: 8, core: 2. Of those that a mesh axis runs over, the one named last changes fastest.
Arguments:
- input_signal: bfloat16 [2, 8192, 1536], P('batch', 'tm'), may hold values from -6 to 6
- standardize_factor: float32 [1536], replicated, may hold values from 0.1 to 1.9
- triple_projection: bfloat16 [3, 1536, 768], P(None, None, 'mp'), may hold values from -0.15625 to 0.15625
- score_sharpening: float32 [8], P('mp'), may hold values from 1 to 3.5
- final_projection: bfloat16 [768, 1536], P('mp'), may hold values from -0.21875 to 0.21875
- filter_taps: float32 [31, 1536], replicated, may hold values from -1.2 to 1.2
- mixture_adjoint: bfloat16 [2, 8192, 1536], P('batch', 'tm'), may hold values from -16 to 16
Outputs:
- sublayer_result: bfloat16 [2, 8192, 1536], P('batch', 'tm')
- signal_adjoint: bfloat16 [2, 8192, 1536], P('batch', 'tm')
- filter_adjoint: float32 [31, 1536], P(None, ('batch', 'tm'))
- amplifier_adjoint: float32 [1536], P(('batch', 'tm'))
All inputs are finite; a program needn't handle non-finite values.
Results may differ from a plain program's by a relative error of at most 0.015.
Values may be sent and summed in bfloat16 or wider, within the bound.
No kernel may reach another device: no remote copies, remote signals or barrier semaphores. Data moves between devices by JAX's collectives and lax.ppermute only.
A program may use at most 128 MiB of HBM per device.

v0:
```python
import math
import jax
import jax.numpy as jnp
from jax import lax
from jax.sharding import PartitionSpec as P

KERNEL = 31


def extended(cells, sides, width):
    for axis, dim in sides:
        count = lax.axis_size(axis)
        ends = count - 1
        head = lax.slice_in_dim(cells, 0, width, axis=dim)
        tail = lax.slice_in_dim(cells, cells.shape[dim] - width, cells.shape[dim], axis=dim)
        cells = jnp.concatenate(
            [
                lax.ppermute(tail, axis, [(i, (i + 1) % count) for i in range(ends)]),
                cells,
                lax.ppermute(head, axis, [((i + 1) % count, i) for i in range(ends)]),
            ],
            axis=dim,
        )
    return cells


def time_rims(field):
    return extended(field, (("tm", 1),), KERNEL // 2)


def heads_total(partial_sum):
    return lax.psum(partial_sum.astype(jnp.bfloat16), "mp").astype(jnp.float32)


def unit_rows(values_in):
    radius = jnp.sqrt(jnp.mean(values_in * values_in, axis=-1, keepdims=True) + 1e-06)
    return (values_in / radius, radius)


def local(
    input_signal,
    standardize_factor,
    triple_projection,
    score_sharpening,
    final_projection,
    filter_taps,
    mixture_adjoint,
):
    rows = input_signal.shape[1]
    resident_subspaces = score_sharpening.shape[0]
    head_breadth = triple_projection.shape[2] // resident_subspaces
    flat_width = resident_subspaces * head_breadth
    taps = filter_taps.shape[0]
    reach = taps // 2
    inputs = input_signal[0].astype(jnp.float32)
    centred = inputs - jnp.mean(inputs, axis=-1, keepdims=True)
    variance = jnp.mean(centred * centred, axis=-1, keepdims=True)
    inverse_std = 1.0 / jnp.sqrt(variance + 1e-05)
    incoming_entries = centred * inverse_std
    normed = (incoming_entries * standardize_factor).astype(jnp.bfloat16)
    query = jnp.dot(normed, triple_projection[0], preferred_element_type=jnp.float32).reshape(
        rows, resident_subspaces, head_breadth
    )
    key_raw = jnp.dot(normed, triple_projection[1], preferred_element_type=jnp.float32).reshape(
        rows, resident_subspaces, head_breadth
    )
    value_raw = jnp.dot(normed, triple_projection[2], preferred_element_type=jnp.float32).reshape(
        rows, resident_subspaces, head_breadth
    )
    normalized_probes, q_radius = unit_rows(query)
    khat, k_radius = unit_rows(key_raw)
    head_sharpening = (score_sharpening / math.sqrt(head_breadth))[None, :, None]
    probe_vectors = (normalized_probes * head_sharpening).astype(jnp.bfloat16)
    keys_local = khat.astype(jnp.bfloat16)
    values_local = value_raw.astype(jnp.bfloat16)
    incoming_adjoint = mixture_adjoint[0].astype(jnp.float32)
    grad_pad = time_rims(mixture_adjoint)[0].astype(jnp.float32)
    grad_res = incoming_adjoint
    for tap_index in range(taps):
        grad_res = (
            grad_res
            + filter_taps[tap_index]
            * grad_pad[2 * reach - tap_index : 2 * reach - tap_index + rows]
        )
    grad_heads = jnp.dot(
        grad_res.astype(jnp.bfloat16), final_projection.T, preferred_element_type=jnp.float32
    )
    grad_heads = grad_heads.astype(jnp.bfloat16).reshape(rows, resident_subspaces, head_breadth)
    zeros_rows = jnp.zeros((rows, resident_subspaces), jnp.float32)
    zeros_full = jnp.zeros((rows, resident_subspaces, head_breadth), jnp.float32)
    start_state = (zeros_rows, zeros_full, zeros_rows, zeros_full, zeros_full)
    key_flat = keys_local.reshape(rows, flat_width)
    value_flat = values_local.reshape(rows, flat_width)
    carry = start_state
    key_piece = lax.all_gather(key_flat, "tm", axis=0, tiled=True)
    value_piece = lax.all_gather(value_flat, "tm", axis=0, tiled=True)
    piece_rows = key_piece.shape[0]
    block_rows = math.gcd(piece_rows, 512)
    block_count = piece_rows // block_rows
    key_blocks = key_piece.reshape(block_count, block_rows, resident_subspaces, head_breadth)
    value_blocks = value_piece.reshape(block_count, block_rows, resident_subspaces, head_breadth)

    def step(state, blocks):
        totals, numer, expect, first, second = state
        key_block, value_block = blocks
        score = jnp.einsum(
            "qhe,khe->qhk", probe_vectors, key_block, preferred_element_type=jnp.float32
        )
        weight = jnp.exp(score)
        weight_low = weight.astype(jnp.bfloat16)
        numer = numer + jnp.einsum(
            "qhk,khe->qhe", weight_low, value_block, preferred_element_type=jnp.float32
        )
        product = jnp.einsum(
            "qhe,khe->qhk", grad_heads, value_block, preferred_element_type=jnp.float32
        )
        weighted = weight * product
        first = first + jnp.einsum(
            "qhk,khe->qhe",
            weighted.astype(jnp.bfloat16),
            key_block,
            preferred_element_type=jnp.float32,
        )
        second = second + jnp.einsum(
            "qhk,khe->qhe", weight_low, key_block, preferred_element_type=jnp.float32
        )
        totals = totals + jnp.sum(weight, axis=-1)
        expect = expect + jnp.sum(weighted, axis=-1)
        return ((totals, numer, expect, first, second), None)

    carry, _ = lax.scan(step, carry, (key_blocks, value_blocks))
    totals, numer, expect, first, second = carry
    attended = (numer / totals[..., None]).astype(jnp.bfloat16)
    deltas = expect / totals
    probe_sensitivity = (first - deltas[..., None] * second) / totals[..., None]
    partial_out = jnp.dot(
        attended.reshape(rows, flat_width), final_projection, preferred_element_type=jnp.float32
    )
    residual = (inputs + heads_total(partial_out)).astype(jnp.bfloat16)
    res_pad = time_rims(residual[None])[0].astype(jnp.float32)
    sublayer_result = residual.astype(jnp.float32)
    filter_pieces = []
    for tap_index in range(taps):
        receptive_span = res_pad[tap_index : tap_index + rows]
        sublayer_result = sublayer_result + filter_taps[tap_index] * receptive_span
        filter_pieces.append(jnp.sum(incoming_adjoint * receptive_span, axis=0))
    sublayer_result = sublayer_result.astype(jnp.bfloat16)
    filter_terms = jnp.stack(filter_pieces)
    carry = (zeros_full, zeros_full)
    query_piece = lax.all_gather(probe_vectors.reshape(rows, flat_width), "tm", axis=0, tiled=True)
    grad_piece = lax.all_gather(grad_heads.reshape(rows, flat_width), "tm", axis=0, tiled=True)
    total_piece = lax.all_gather(totals.astype(jnp.bfloat16), "tm", axis=0, tiled=True).astype(
        jnp.float32
    )
    delta_piece = lax.all_gather(deltas.astype(jnp.bfloat16), "tm", axis=0, tiled=True).astype(
        jnp.float32
    )
    piece_rows = query_piece.shape[0]
    block_rows = math.gcd(piece_rows, 512)
    block_count = piece_rows // block_rows
    query_blocks = query_piece.reshape(block_count, block_rows, resident_subspaces, head_breadth)
    grad_blocks = grad_piece.reshape(block_count, block_rows, resident_subspaces, head_breadth)
    total_blocks = total_piece.reshape(block_count, block_rows, resident_subspaces)
    delta_blocks = delta_piece.reshape(block_count, block_rows, resident_subspaces)

    def step(state, blocks):
        key_sum, value_sum = state
        query_block, grad_block, total_block, delta_block = blocks
        score = jnp.einsum(
            "khe,qhe->khq", keys_local, query_block, preferred_element_type=jnp.float32
        )
        prob = jnp.exp(score) / total_block.T[None]
        value_sum = value_sum + jnp.einsum(
            "khq,qhe->khe",
            prob.astype(jnp.bfloat16),
            grad_block,
            preferred_element_type=jnp.float32,
        )
        product = jnp.einsum(
            "khe,qhe->khq", values_local, grad_block, preferred_element_type=jnp.float32
        )
        slope = prob * (product - delta_block.T[None])
        key_sum = key_sum + jnp.einsum(
            "khq,qhe->khe",
            slope.astype(jnp.bfloat16),
            query_block,
            preferred_element_type=jnp.float32,
        )
        return ((key_sum, value_sum), None)

    carry, _ = lax.scan(step, carry, (query_blocks, grad_blocks, total_blocks, delta_blocks))
    grad_keys, grad_values = carry
    sharpened_sensitivity = probe_sensitivity * head_sharpening
    query_grad = (
        sharpened_sensitivity
        - normalized_probes
        * jnp.mean(sharpened_sensitivity * normalized_probes, axis=-1, keepdims=True)
    ) / q_radius
    key_grad = (grad_keys - khat * jnp.mean(grad_keys * khat, axis=-1, keepdims=True)) / k_radius
    normed_part = jnp.dot(
        query_grad.astype(jnp.bfloat16).reshape(rows, flat_width),
        triple_projection[0].T,
        preferred_element_type=jnp.float32,
    )
    normed_part = normed_part + jnp.dot(
        key_grad.astype(jnp.bfloat16).reshape(rows, flat_width),
        triple_projection[1].T,
        preferred_element_type=jnp.float32,
    )
    normed_part = normed_part + jnp.dot(
        grad_values.astype(jnp.bfloat16).reshape(rows, flat_width),
        triple_projection[2].T,
        preferred_element_type=jnp.float32,
    )
    standardized_adjoint = heads_total(normed_part)
    amplifier_terms = jnp.sum(standardized_adjoint * incoming_entries, axis=0)
    scaled = standardized_adjoint * standardize_factor
    frame_back = (
        scaled
        - jnp.mean(scaled, axis=-1, keepdims=True)
        - incoming_entries * jnp.mean(scaled * incoming_entries, axis=-1, keepdims=True)
    ) * inverse_std
    signal_adjoint = (grad_res + frame_back).astype(jnp.bfloat16)
    kernel_part, gain_part = (
        lax.psum_scatter(filter_terms, ("batch", "tm"), scatter_dimension=1, tiled=True),
        lax.psum_scatter(amplifier_terms, ("batch", "tm"), scatter_dimension=0, tiled=True),
    )
    return (sublayer_result[None], signal_adjoint[None], kernel_part, gain_part)


def solution(mesh):
    return jax.shard_map(
        local,
        mesh=mesh,
        in_specs=(
            P("batch", "tm", None),
            P(),
            P(None, None, "mp"),
            P("mp"),
            P("mp", None),
            P(),
            P("batch", "tm", None),
        ),
        out_specs=(
            P("batch", "tm", None),
            P("batch", "tm", None),
            P(None, ("batch", "tm")),
            P(("batch", "tm")),
        ),
        check_vma=False,
    )
```

profile of v0, /device:TPU:2, one launch (start us, length us, event | category | flops | bytes accessed | tf_op | source)
XLA Modules:
  0.0 1526.4 jit_solution(12637345963958603732)
XLA Ops:
  9.7 3.8 slice_bitcast_fusion
  13.5 2.4 copy.43
  19.2 2.4 copy.45
  21.7 2.5 convolution_convert_fusion.2
  28.5 5.1 collective-permute-start
  33.6 3.1 collective-permute-start.1
  37.7 3.6 collective-permute-done.1
  41.4 3.1 fusion.132
  46.6 94.8 %all-gather.5.cloned.1.call-done = bf16[8192,384]{0,1:T(8,128)(2,1)} async-done(((bf16[128,384]{0,1:T(8,128)(2,1)}), bf16[8192,384]{0,1:T(8,128)(2,1)}) %all-gather.5.cloned.1.call-update) | async-done | bytes 6291472 | tf_op jit(solution)/shard_map/all_gather | solution.py:95
  141.4 5.7 copy.62
  147.1 6.3 copy.47
  153.5 111.7 %all-gather.7.cloned.1.call-done = bf16[8192,384]{0,1:T(8,128)(2,1)} async-done(((bf16[128,384]{0,1:T(8,128)(2,1)}), bf16[8192,384]{0,1:T(8,128)(2,1)}) %all-gather.7.cloned.1.call-update) | async-done | bytes 6291472 | tf_op jit(solution)/shard_map/all_gather | solution.py:96
  265.1 5.7 copy.63
  270.8 16.8 %copy.48 = bf16[16,512,4,96]{1,3,2,0:T(8,128)(2,1)} copy(bf16[16,512,4,96]{1,0,3,2:T(8,128)(2,1)S(1)} %bitcast.714) | data formatting | bytes 12582912
  287.6 128.9 %while.32 = (s32[]{:T(128)}, f32[128,4]{0,1:T(4,128)S(1)}, f32[128,4,96]{0,2,1:T(8,128)}, f32[128,4]{0,1:T(4,128)S(1)}, f32[128,4,96]{0,2,1:T(8,128)}, /*index=5...) while((s32[]{:T(128)}, f32[128,4]{0,1:T(4,128)S(1)}, ...), condition=%wide.region_7.8_spmd.clone, body=%wide.region_4.7_spmd.clone.sunk | while | flops 253527040 | bytes 8997542 | solution.py:131
  290.4 1.9 fusion.231
  293.6 1.9 fusion.230
  298.3 2.0 fusion.231
  301.6 2.0 fusion.230
  306.4 2.0 fusion.231
  309.7 2.0 fusion.230
  314.4 2.0 fusion.231
  317.7 2.0 fusion.230
  322.5 2.0 fusion.231
  325.8 2.0 fusion.230
  330.5 2.0 fusion.231
  333.8 2.0 fusion.230
  338.6 2.0 fusion.231
  341.9 2.0 fusion.230
  346.6 2.0 fusion.231
  350.0 2.0 fusion.230
  354.7 2.0 fusion.231
  358.0 2.0 fusion.230
  362.8 2.0 fusion.231
  366.1 2.0 fusion.230
  370.9 2.0 fusion.231
  374.2 2.0 fusion.230
  379.0 2.0 fusion.231
  382.3 2.0 fusion.230
  387.1 2.0 fusion.231
  390.4 2.0 fusion.230
  395.1 2.0 fusion.231
  398.4 2.0 fusion.230
  403.2 2.0 fusion.231
  406.5 2.0 fusion.230
  411.2 2.0 fusion.231
  414.5 2.0 fusion.230
  416.5 177.8 %all_gather.21 = bf16[8192,4]{0,1:T(4,128)(2,1)S(1)} all-gather(bf16[128,4]{0,1:T(4,128)(2,1)S(1)} %get-tuple-element.367), channel_id=1, replica_groups=mesh['batch'=2,'tm'=64,'mp'=2] {'tm'}, dimensions={0}, use_global_device_ids=true | all-gather | bytes 66560 | tf_op jit(solution)/shard_map/all_gather | solution.py:152
  594.4 174.2 %all_gather.23 = bf16[8192,4]{0,1:T(4,128)(2,1)S(1)} all-gather(bf16[128,4]{0,1:T(4,128)(2,1)S(1)} %get-tuple-element.348), channel_id=1, replica_groups=mesh['batch'=2,'tm'=64,'mp'=2] {'tm'}, dimensions={0}, use_global_device_ids=true | all-gather | bytes 66560 | tf_op jit(solution)/shard_map/all_gather | solution.py:155
  768.6 5.7 copy.64
  774.4 6.4 copy.50
  783.9 16.0 %reshape.263 = bf16[16,512,4,96]{3,2,1,0:T(4,128)(2,1)} reshape(bf16[8192,384]{1,0:T(8,128)(2,1)} %all-gather.11.cloned.1.call-done) | data formatting | bytes 12582912 | tf_op jit(solution)/shard_map/reshape | solution.py:162
  800.0 13.3 copy.51
  813.2 75.2 %while.33 = (s32[]{:T(128)}, f32[128,4,96]{0,2,1:T(8,128)S(1)}, f32[128,4,96]{0,2,1:T(8,128)S(1)}, bf16[16,512,4,96]{1,3,2,0:T(8,128)(2,1)}, bf16[128,4,96]{0,2,...) while((s32[]{:T(128)}, f32[128,4,96]{0,2,1:T(8,128)S(1)}, ...), condition=%wide.region_11.12_spmd.clone, body=%wide.region_10.11_spmd.clone.sunk | while | flops 202833920 | bytes 5752956 | solution.py:191
  890.5 2.5 fusion.48
  893.2 30.2 %all-reduce.8.cloned.1.call-done = (bf16[128,1536]{1,0:T(8,128)(2,1)}, bf16[128,1536]{1,0:T(8,128)(2,1)}) async-done(((bf16[128,1536]{1,0:T(8,128)(2,1)}, bf16[128,1536]{1,0:T(8,128)(2,1)}), (bf16[128,1536]{1,0:T(8,128)(2,1)}, bf16[128,1536]{1,0:T(8,128)(2,1)})) %all-reduce.8.cloned.1.call-update) | async-done | bytes 786448 | tf_op jit(solution)/shard_map/psum | solution.py:32
  924.9 2.3 fusion.168
  927.2 4.9 collective-permute-start.2
  932.1 3.3 collective-permute-start.3
  936.7 349.4 %all-reduce.1 = f32[1536]{0:T(1024)S(1)} all-reduce(f32[1536]{0:T(1024)S(1)} %get-tuple-element.274), channel_id=3, replica_groups=mesh['batch'=2,'tm'=64,'mp'=2] {'batch','tm'}, use_global_device_ids=true, to_apply=%region_49.50.clone | all-reduce | flops 1536 | bytes 12288
  1286.8 2.0 fusion.130
  1290.6 2.7 stack.127
  1293.7 4.7 fusion.170
  1298.4 219.4 %all-reduce.6.cloned.1.call-done = f32[31,1536]{1,0:T(8,128)} async-done(((f32[31,1536]{1,0:T(8,128)}), f32[31,1536]{1,0:T(8,128)}) %all-reduce.6.cloned.1.call-update) | async-done | bytes 190480
  (437 shorter events, 163.2 us)
Async XLA Ops:
  7.2 37.7 %copy-start = (bf16[384,1536]{1,0:T(8,128)(2,1)S(1)}, bf16[384,1536]{1,0:T(8,128)(2,1)}, u32[]{:S(2)}) copy-start(bf16[384,1536]{1,0:T(8,128)(2,1)} %param.15) | copy-start | bytes 3538948
  7.2 134.2 %all-gather.5.cloned.1.call-start = ((), (), s32[]{:S(2)}) async-start(), calls=%async_computation | async-start | bytes 6389760 | tf_op jit(solution)/shard_map/all_gather | solution.py:95
  8.5 17.4 %copy-start.86 = (f32[128]{0:T(128)}, f32[128]{0:T(128)S(1)}, u32[]{:S(2)}) copy-start(f32[128]{0:T(128)S(1)} %broadcast_multiply_fusion.5) | copy-start | bytes 1540
  9.7 16.1 %copy-start.88 = (f32[128]{0:T(128)}, f32[128]{0:T(128)S(1)}, u32[]{:S(2)}) copy-start(f32[128]{0:T(128)S(1)} %add_rsqrt_fusion) | copy-start | bytes 1540
  18.5 7.3 copy-start.90
  19.2 246.0 %all-gather.7.cloned.1.call-start = ((), (), s32[]{:S(2)}) async-start(), calls=%async_computation.1 | async-start | bytes 6389760 | tf_op jit(solution)/shard_map/all_gather | solution.py:96
  21.6 6.9 copy-start.4
  21.6 15.1 copy-start.20
  24.2 744.4 %all-gather.9.cloned.1.call-start = ((), (), s32[]{:S(2)}) async-start(), calls=%async_computation.2 | async-start | bytes 6389760 | tf_op jit(solution)/shard_map/all_gather | solution.py:150
  27.7 13.8 copy-start.13
  28.4 755.5 %all-gather.11.cloned.1.call-start = ((), (), s32[]{:S(2)}) async-start(), calls=%async_computation.3 | async-start | bytes 6389760 | tf_op jit(solution)/shard_map/all_gather | solution.py:151
  28.5 9.2 collective-permute-start
  33.6 7.7 collective-permute-start.1
  37.1 7.4 copy-start.21
  37.1 7.4 copy-start.23
  37.1 7.4 copy-start.25
  37.2 7.4 copy-start.27
  37.2 7.4 copy-start.29
  37.2 7.4 copy-start.31
  37.2 7.4 copy-start.33
  37.2 7.4 copy-start.35
  37.2 7.4 copy-start.37
  37.2 7.4 copy-start.39
  37.2 7.4 copy-start.41
  37.2 7.4 copy-start.43
  37.2 7.4 copy-start.45
  37.3 7.4 copy-start.47
  37.3 7.4 copy-start.49
  37.3 7.4 copy-start.51
  37.3 7.4 copy-start.53
  37.3 7.4 copy-start.55
  37.3 7.4 copy-start.57
  37.5 7.2 copy-start.59
  37.5 7.2 copy-start.61
  37.5 7.2 copy-start.63
  37.5 7.2 copy-start.65
  37.6 7.2 copy-start.67
  37.6 7.2 copy-start.69
  37.6 7.2 copy-start.71
  37.6 7.2 copy-start.73
  37.6 7.2 copy-start.74
  37.6 7.2 copy-start.75
  37.6 7.2 copy-start.76
  37.6 7.2 copy-start.77
  44.9 102.3 %copy-start.8 = (f32[128,1536]{1,0:T(8,128)}, f32[128,1536]{1,0:T(8,128)S(1)}, u32[]{:S(2)}) copy-start(f32[128,1536]{1,0:T(8,128)S(1)} %fusion.132) | copy-start | bytes 2359300
  46.2 877.3 %all-reduce.8.cloned.1.call-start = ((), (), s32[]{:S(2)}) async-start(), calls=%async_computation.5 | async-start | bytes 1572864 | tf_op jit(solution)/shard_map/psum | solution.py:32
  270.8 16.8 %copy-start.10 = (bf16[128,4,96]{0,2,1:T(8,128)(2,1)S(1)}, bf16[128,4,96]{0,2,1:T(8,128)(2,1)}, u32[]{:S(2)}) copy-start(bf16[128,4,96]{0,2,1:T(8,128)(2,1)} %multiply_convert_fusion) | copy-start | bytes 294916
  774.3 6.4 copy-start.3
  774.4 6.5 copy-start.7
  799.9 13.3 copy-start.6
  799.9 13.3 copy-start.12
  799.9 13.3 copy-start.19
  813.2 75.2 %copy-start.16 = (f32[128,4,96]{0,2,1:T(8,128)S(1)}, f32[128,4,96]{0,2,1:T(8,128)}, u32[]{:S(2)}) copy-start(f32[128,4,96]{0,2,1:T(8,128)} %copy-done.15) | copy-start | bytes 589828
  813.2 75.2 %copy-start.81 = (f32[128,4]{0,1:T(4,128)S(1)}, f32[128,4]{0,1:T(4,128)}, u32[]{:S(2)}) copy-start(f32[128,4]{0,1:T(4,128)} %copy-done.80) | copy-start | bytes 6148
  888.5 35.0 %copy-start.79 = (f32[1536]{0:T(1024)S(1)}, f32[1536]{0:T(1024)}, u32[]{:S(2)}) copy-start(f32[1536]{0:T(1024)} %param.12) | copy-start | bytes 18436
  888.5 35.0 %copy-start.87 = (f32[128]{0:T(128)S(1)}, f32[128]{0:T(128)}, u32[]{:S(2)}) copy-start(f32[128]{0:T(128)} %copy-done.86) | copy-start | bytes 1540
  888.5 35.0 %copy-start.89 = (f32[128]{0:T(128)S(1)}, f32[128]{0:T(128)}, u32[]{:S(2)}) copy-start(f32[128]{0:T(128)} %copy-done.88) | copy-start | bytes 1540
  888.6 36.3 %copy-start.9 = (f32[128,1536]{1,0:T(8,128)S(1)}, f32[128,1536]{1,0:T(8,128)}, u32[]{:S(2)}) copy-start(f32[128,1536]{1,0:T(8,128)} %copy-done.8) | copy-start | bytes 2359300
  890.4 45.0 %copy-start.91 = (u32[256]{0:T(256)S(1)}, u32[256]{0:T(256)}, u32[]{:S(2)}) copy-start(u32[256]{0:T(256)} %constant.50) | copy-start | bytes 3076
  893.0 393.8 %copy-start.5 = (bf16[1,128,1536]{2,1,0:T(8,128)(2,1)S(1)}, bf16[1,128,1536]{2,1,0:T(8,128)(2,1)}, u32[]{:S(2)}) copy-start(bf16[1,128,1536]{2,1,0:T(8,128)(2,1)} %param.17) | copy-start | bytes 1179652
  893.0 624.8 %all-reduce.6.cloned.1.call-start = ((), (), s32[]{:S(2)}) async-start(), calls=%async_computation.4 | async-start | bytes 393216
  927.2 359.5 %collective-permute-start.2 = (bf16[1,15,1536]{2,1,0:T(8,128)(2,1)S(1)}, bf16[1,15,1536]{2,1,0:T(8,128)(2,1)S(1)}, u32[]{:S(2)}, u32[]{:S(2)}) collective-permute-start(bf16[1,15,1536]{2,1,0:T(8,128)(2,1)S(1)} %get-tuple-element.363), channel_id=1, source_target_pairs={{0,2},{2,4},{4,6},{6,8},{8,10},{10,12},{12,14},{14,16},{16,18},{18... | collective-permute-start | bytes 138248 | tf_op jit(solution)/shard_map/ppermute | solution.py:18
  932.1 354.5 %collective-permute-start.3 = (bf16[1,15,1536]{2,1,0:T(8,128)(2,1)S(1)}, bf16[1,15,1536]{2,1,0:T(8,128)(2,1)S(1)}, u32[]{:S(2)}, u32[]{:S(2)}) collective-permute-start(bf16[1,15,1536]{2,1,0:T(8,128)(2,1)S(1)} %get-tuple-element.364), channel_id=1, source_target_pairs={{2,0},{4,2},{6,4},{8,6},{10,8},{12,10},{14,12},{16,14},{18,16},{20... | collective-permute-start | bytes 138248 | tf_op jit(solution)/shard_map/ppermute | solution.py:20
  1293.7 225.6 %copy-start.1 = (bf16[384,1536]{1,0:T(8,128)(2,1)S(1)}, bf16[384,1536]{1,0:T(8,128)(2,1)}, u32[]{:S(2)}) copy-start(bf16[384,1536]{1,0:T(8,128)(2,1)} %param.15) | copy-start | bytes 3538948
  (53 other events, 217.2 us)
Sparse Core Ops, SparseCore 0:
  19.3 122.1 all-gather.4
  144.9 120.2 all-gather.6
  268.6 120.2 all-gather.8
  392.4 138.0 all-gather.10
  893.1 30.2 all-reduce.7
  1293.5 224.1 all-reduce.5
where the time goes:
time: 1540 us; the launch traced here: 1530 us
  blocking collectives  701 us (46%)
  waiting for transfers between devices  460 us (30%)
  matrix products  217 us (14%)
  local copies, waits for them, and re-layouts  94.1 us (6%)
  other arithmetic  19.3 us (1%)
  starting transfers between devices  17.3 us (1%)
  between operations  16.8 us (1%)
    unnamed x1, blocking collectives  349 us
    unnamed x7, waiting for transfers between devices  219 us
    all_gather x1, blocking collectives, local(): lax.all_gather(totals.astype(jnp.bfloat16), 'tm', axis=0, tiled=True)  178 us
    all_gather x1, blocking collectives, local(): lax.all_gather(deltas.astype(jnp.bfloat16), 'tm', axis=0, tiled=True)  174 us
    all_gather x1, waiting for transfers between devices, local(): value_piece = lax.all_gather(value_flat, 'tm', axis=0, tiled=True)  112 us
    all_gather x1, waiting for transfers between devices, local(): key_piece = lax.all_gather(key_flat, 'tm', axis=0, tiled=True)  94.8 us
    unnamed x193, local copies, waits for them, and re-layouts  63.6 us
    dot_general x16, matrix products, step(): jnp.einsum('qhk,khe->qhe', weight_low, value_block, preferred_element_typ...  31.8 us
  transfers between devices with their start and end apart: 10, of which 5 were waited for; matrix products, arithmetic and copies ran while one was open for 13% of the time, Pallas kernels for 0%

commit v1 on v0

--- a/solution.py
+++ b/solution.py
@@ -92,8 +92,11 @@
     key_flat = keys_local.reshape(rows, flat_width)
     value_flat = values_local.reshape(rows, flat_width)
     carry = start_state
-    key_piece = lax.all_gather(key_flat, "tm", axis=0, tiled=True)
-    value_piece = lax.all_gather(value_flat, "tm", axis=0, tiled=True)
+    key_piece, value_piece = jnp.split(
+        lax.all_gather(jnp.concatenate([key_flat, value_flat], axis=1), "tm", axis=0, tiled=True),
+        [key_flat.shape[1]],
+        axis=1,
+    )
     piece_rows = key_piece.shape[0]
     block_rows = math.gcd(piece_rows, 512)
     block_count = piece_rows // block_rows

time: 1540 us -> 1690 us (1.097)
  waiting for transfers between devices: 460 us -> 609 us
    all_gather x1, waiting for transfers between devices: 0.02 us -> 130 us  [local(): lax.all_gather(grad_heads.reshape(rows, flat_width), 'tm', axis=0, tiled=...]
    all_gather x1, waiting for transfers between devices: 0.02 us -> 92.6 us  [local(): lax.all_gather(probe_vectors.reshape(rows, flat_width), 'tm', axis=0, til...]
    all_gather x2 -> x1, waiting for transfers between devices: 206 us -> 126 us  [local(): lax.all_gather(jnp.concatenate([key_flat, value_flat], axis=1), 'tm', axi...]
    unnamed x193 -> x177, local copies, waits for them, and re-layouts: 63.6 us -> 50.3 us
    unnamed x7 -> x6, waiting for transfers between devices: 219 us -> 224 us
  transfers between devices with their start and end apart: 10 -> 9, of which waited for: 5 -> 6; matrix products, arithmetic and copies ran while one was open for 13% -> 4% of each run, Pallas kernels for 0% -> 0%
where the time goes in v1:
time: 1690 us; the launch traced here: 1680 us
  blocking collectives  697 us (41%)
  waiting for transfers between devices  609 us (36%)
  matrix products  217 us (13%)
  local copies, waits for them, and re-layouts  101 us (6%)
  other arithmetic  20.8 us (1%)
    unnamed x1, blocking collectives  347 us
    unnamed x6, waiting for transfers between devices  224 us
    all_gather x1, blocking collectives, local(): lax.all_gather(totals.astype(jnp.bfloat16), 'tm', axis=0, tiled=True)  176 us
    all_gather x1, blocking collectives, local(): lax.all_gather(deltas.astype(jnp.bfloat16), 'tm', axis=0, tiled=True)  174 us
    all_gather x1, waiting for transfers between devices, local(): lax.all_gather(grad_heads.reshape(rows, flat_width), 'tm', axis=0, tiled=...  130 us
    all_gather x1, waiting for transfers between devices, local(): lax.all_gather(jnp.concatenate([key_flat, value_flat], axis=1), 'tm', axi...  126 us
    all_gather x1, waiting for transfers between devices, local(): lax.all_gather(probe_vectors.reshape(rows, flat_width), 'tm', axis=0, til...  92.6 us
    unnamed x177, local copies, waits for them, and re-layouts  50.3 us
  transfers between devices with their start and end apart: 9, of which 6 were waited for; matrix products, arithmetic and copies ran while one was open for 4% of the time, Pallas kernels for 0%

profile of v1, /device:TPU:2, one launch (start us, length us, event | category | flops | bytes accessed | tf_op | source)
XLA Modules:
  0.0 1678.3 jit_solution(6459833492583470057)
XLA Ops:
  7.2 3.8 slice_bitcast_fusion
  16.3 5.1 collective-permute-start.1
  21.4 2.3 collective-permute-start
  24.6 5.3 collective-permute-done
  29.9 3.1 fusion.132
  34.6 2.4 copy.44
  37.0 2.5 copy.43
  45.9 92.6 %all-gather.6.cloned.1.call-done = bf16[8192,384]{0,1:T(8,128)(2,1)} async-done(((bf16[128,384]{0,1:T(8,128)(2,1)}), bf16[8192,384]{0,1:T(8,128)(2,1)}) %all-gather.6.cloned.1.call-update) | async-done | bytes 6291472 | tf_op jit(solution)/shard_map/all_gather | solution.py:153
  138.5 5.7 copy.64
  144.2 6.3 copy.50
  150.6 129.5 %all-gather.8.cloned.1.call-done = bf16[8192,384]{1,0:T(8,128)(2,1)} async-done(((bf16[128,384]{1,0:T(8,128)(2,1)}), bf16[8192,384]{1,0:T(8,128)(2,1)}) %all-gather.8.cloned.1.call-update) | async-done | bytes 6291472 | tf_op jit(solution)/shard_map/all_gather | solution.py:154
  280.1 16.0 reshape.263
  296.1 13.2 copy.51
  309.2 126.5 %all-gather.4.cloned.1.call-done = bf16[8192,768]{0,1:T(8,128)(2,1)} async-done(((bf16[128,768]{0,1:T(8,128)(2,1)}), bf16[8192,768]{0,1:T(8,128)(2,1)}) %all-gather.4.cloned.1.call-update) | async-done | bytes 12582928 | tf_op jit(solution)/shard_map/all_gather | solution.py:96
  435.7 8.7 fusion.181
  444.4 5.7 copy.62
  450.1 6.3 copy.47
  456.4 2.9 copy.63
  459.4 6.5 copy.48
  465.8 128.6 %while.32 = (s32[]{:T(128)}, f32[128,4]{0,1:T(4,128)S(1)}, f32[128,4,96]{0,2,1:T(8,128)}, f32[128,4]{0,1:T(4,128)S(1)}, f32[128,4,96]{0,2,1:T(8,128)}, /*index=5...) while((s32[]{:T(128)}, f32[128,4]{0,1:T(4,128)S(1)}, ...), condition=%wide.region_7.8_spmd.clone, body=%wide.region_4.7_spmd.clone.sunk | while | flops 253527040 | bytes 8601758 | solution.py:134
  476.6 2.0 fusion.231
  478.6 2.0 fusion.232
  484.6 2.0 fusion.231
  486.6 2.0 fusion.232
  492.7 2.0 fusion.231
  494.7 2.0 fusion.232
  500.7 2.0 fusion.231
  502.7 2.0 fusion.232
  508.7 2.0 fusion.231
  510.7 2.0 fusion.232
  516.8 2.0 fusion.231
  518.8 2.0 fusion.232
  524.8 2.0 fusion.231
  526.8 2.0 fusion.232
  532.9 2.0 fusion.231
  534.9 2.0 fusion.232
  540.9 2.0 fusion.231
  542.9 2.0 fusion.232
  549.0 2.0 fusion.231
  550.9 2.0 fusion.232
  557.0 2.0 fusion.231
  559.0 2.0 fusion.232
  565.0 2.0 fusion.231
  567.0 2.0 fusion.232
  573.1 2.0 fusion.231
  575.1 2.0 fusion.232
  581.1 2.0 fusion.231
  589.2 2.0 fusion.231
  591.2 2.0 fusion.232
  598.0 2.7 fusion.49
  600.7 175.9 %all_gather.17 = bf16[8192,4]{0,1:T(4,128)(2,1)S(1)} all-gather(bf16[128,4]{0,1:T(4,128)(2,1)S(1)} %get-tuple-element.369), channel_id=1, replica_groups=mesh['batch'=2,'tm'=64,'mp'=2] {'tm'}, dimensions={0}, use_global_device_ids=true | all-gather | bytes 66560 | tf_op jit(solution)/shard_map/all_gather | solution.py:155
  776.6 174.2 %all_gather.19 = bf16[8192,4]{0,1:T(4,128)(2,1)S(1)} all-gather(bf16[128,4]{0,1:T(4,128)(2,1)S(1)} %get-tuple-element.348), channel_id=1, replica_groups=mesh['batch'=2,'tm'=64,'mp'=2] {'tm'}, dimensions={0}, use_global_device_ids=true | all-gather | bytes 66560 | tf_op jit(solution)/shard_map/all_gather | solution.py:158
  951.5 86.3 %while.33 = (s32[]{:T(128)}, f32[128,4,96]{0,2,1:T(8,128)S(1)}, f32[128,4,96]{0,2,1:T(8,128)S(1)}, bf16[16,512,4,96]{1,3,2,0:T(8,128)(2,1)}, bf16[128,4,96]{0,2,...) while((s32[]{:T(128)}, f32[128,4,96]{0,2,1:T(8,128)S(1)}, ...), condition=%wide.region_11.12_spmd.clone, body=%wide.region_10.11_spmd.clone.sunk | while | flops 202833920 | bytes 5752459 | solution.py:194
  1038.0 2.1 convolution_add_fusion.1
  1040.1 2.5 fusion.48
  1042.7 31.3 %all-reduce.8.cloned.1.call-done = (bf16[128,1536]{1,0:T(8,128)(2,1)}, bf16[128,1536]{1,0:T(8,128)(2,1)}) async-done(((bf16[128,1536]{1,0:T(8,128)(2,1)}, bf16[128,1536]{1,0:T(8,128)(2,1)}), (bf16[128,1536]{1,0:T(8,128)(2,1)}, bf16[128,1536]{1,0:T(8,128)(2,1)})) %all-reduce.8.cloned.1.call-update) | async-done | bytes 786448 | tf_op jit(solution)/shard_map/psum | solution.py:32
  1075.4 2.3 fusion.168
  1077.7 4.9 collective-permute-start.3
  1082.6 2.4 collective-permute-start.2
  1086.3 347.3 %all-reduce.1 = f32[1536]{0:T(1024)S(1)} all-reduce(f32[1536]{0:T(1024)S(1)} %get-tuple-element.274), channel_id=3, replica_groups=mesh['batch'=2,'tm'=64,'mp'=2] {'batch','tm'}, use_global_device_ids=true, to_apply=%region_49.50.clone | all-reduce | flops 1536 | bytes 12288
  1434.3 2.2 fusion.130
  1438.4 2.7 stack.127
  1441.4 4.6 fusion.170
  1446.0 224.0 %all-reduce.6.cloned.1.call-done = f32[31,1536]{1,0:T(8,128)} async-done(((f32[31,1536]{1,0:T(8,128)}), f32[31,1536]{1,0:T(8,128)}) %all-reduce.6.cloned.1.call-update) | async-done | bytes 190480
  (388 shorter events, 179.7 us)
Async XLA Ops:
  7.2 26.2 %copy-start = (bf16[384,1536]{1,0:T(8,128)(2,1)S(1)}, bf16[384,1536]{1,0:T(8,128)(2,1)}, u32[]{:S(2)}) copy-start(bf16[384,1536]{1,0:T(8,128)(2,1)} %param.15) | copy-start | bytes 3538948
  7.2 5.5 copy-start.1
  7.2 6.4 copy-start.73
  7.2 131.3 %all-gather.6.cloned.1.call-start = ((), (), s32[]{:S(2)}) async-start(), calls=%async_computation.1 | async-start | bytes 6389760 | tf_op jit(solution)/shard_map/all_gather | solution.py:153
  11.1 5.2 copy-start.2
  11.1 12.6 copy-start.15
  12.8 28.7 %copy-start.79 = (f32[128]{0:T(128)}, f32[128]{0:T(128)S(1)}, u32[]{:S(2)}) copy-start(f32[128]{0:T(128)S(1)} %broadcast_multiply_fusion.5) | copy-start | bytes 1540
  15.4 14.5 copy-start.9
  16.3 263.8 %all-gather.8.cloned.1.call-start = ((), (), s32[]{:S(2)}) async-start(), calls=%async_computation.2 | async-start | bytes 6389760 | tf_op jit(solution)/shard_map/all_gather | solution.py:154
  16.3 8.2 collective-permute-start.1
  21.4 8.4 collective-permute-start
  24.0 9.0 copy-start.16
  24.0 9.0 copy-start.18
  24.0 9.0 copy-start.20
  24.1 9.0 copy-start.22
  24.1 9.0 copy-start.24
  24.1 9.0 copy-start.26
  24.1 9.0 copy-start.28
  24.1 9.0 copy-start.30
  24.1 9.0 copy-start.32
  24.1 9.0 copy-start.34
  24.1 9.0 copy-start.36
  24.1 9.0 copy-start.38
  24.1 9.0 copy-start.40
  24.2 9.0 copy-start.42
  24.2 9.0 copy-start.44
  24.2 9.0 copy-start.46
  24.2 9.0 copy-start.48
  24.2 9.0 copy-start.50
  24.2 9.0 copy-start.52
  24.4 8.8 copy-start.54
  24.4 8.8 copy-start.56
  24.4 8.8 copy-start.58
  24.4 8.8 copy-start.60
  24.5 8.8 copy-start.62
  24.5 8.8 copy-start.64
  24.5 8.8 copy-start.66
  24.5 8.8 copy-start.68
  24.5 8.8 copy-start.69
  24.5 8.8 copy-start.70
  24.5 8.8 copy-start.71
  24.5 8.8 copy-start.72
  33.4 8.0 copy-start.5
  34.6 401.1 %all-gather.4.cloned.1.call-start = ((), (), s32[]{:S(2)}) async-start(), calls=%async_computation | async-start | bytes 12779520 | tf_op jit(solution)/shard_map/all_gather | solution.py:96
  37.0 8.1 copy-start.13
  41.4 102.8 %copy-start.10 = (f32[128,4,96]{0,2,1:T(8,128)}, f32[128,4,96]{0,2,1:T(8,128)S(1)}, u32[]{:S(2)}) copy-start(f32[128,4,96]{0,2,1:T(8,128)S(1)} %get-tuple-element.373) | copy-start | bytes 589828
  41.5 102.8 %copy-start.14 = (bf16[128,4,96]{0,2,1:T(8,128)(2,1)}, bf16[128,4,96]{0,2,1:T(8,128)(2,1)S(1)}, u32[]{:S(2)}) copy-start(bf16[128,4,96]{0,2,1:T(8,128)(2,1)S(1)} %fusion.172) | copy-start | bytes 294916
  44.7 1029.2 %all-reduce.8.cloned.1.call-start = ((), (), s32[]{:S(2)}) async-start(), calls=%async_computation.4 | async-start | bytes 1572864 | tf_op jit(solution)/shard_map/psum | solution.py:32
  594.4 357.1 %copy-start.4 = (f32[128,4,96]{0,2,1:T(8,128)S(1)}, f32[128,4,96]{0,2,1:T(8,128)}, u32[]{:S(2)}) copy-start(f32[128,4,96]{0,2,1:T(8,128)} %custom-call.6) | copy-start | bytes 589828
  594.4 357.1 %copy-start.8 = (bf16[128,4,96]{0,2,1:T(8,128)(2,1)S(1)}, bf16[128,4,96]{0,2,1:T(8,128)(2,1)}, u32[]{:S(2)}) copy-start(bf16[128,4,96]{0,2,1:T(8,128)(2,1)} %copy-done.7) | copy-start | bytes 294916
  951.5 86.3 %copy-start.11 = (f32[128,4,96]{0,2,1:T(8,128)S(1)}, f32[128,4,96]{0,2,1:T(8,128)}, u32[]{:S(2)}) copy-start(f32[128,4,96]{0,2,1:T(8,128)} %copy-done.10) | copy-start | bytes 589828
  951.5 86.3 %copy-start.77 = (f32[128,4]{0,1:T(4,128)S(1)}, f32[128,4]{0,1:T(4,128)}, u32[]{:S(2)}) copy-start(f32[128,4]{0,1:T(4,128)} %copy-done.76) | copy-start | bytes 6148
  1037.9 36.1 %copy-start.74 = (f32[1536]{0:T(1024)S(1)}, f32[1536]{0:T(1024)}, u32[]{:S(2)}) copy-start(f32[1536]{0:T(1024)} %param.12) | copy-start | bytes 18436
  1037.9 36.1 %copy-start.80 = (f32[128]{0:T(128)S(1)}, f32[128]{0:T(128)}, u32[]{:S(2)}) copy-start(f32[128]{0:T(128)} %copy-done.79) | copy-start | bytes 1540
  1038.0 37.4 %copy-start.6 = (f32[128,1536]{1,0:T(8,128)S(1)}, f32[128,1536]{1,0:T(8,128)}, u32[]{:S(2)}) copy-start(f32[128,1536]{1,0:T(8,128)} %copy-done.5) | copy-start | bytes 2359300
  1040.1 45.0 %copy-start.82 = (u32[256]{0:T(256)S(1)}, u32[256]{0:T(256)}, u32[]{:S(2)}) copy-start(u32[256]{0:T(256)} %constant.50) | copy-start | bytes 3076
  1042.6 391.7 %copy-start.3 = (bf16[1,128,1536]{2,1,0:T(8,128)(2,1)S(1)}, bf16[1,128,1536]{2,1,0:T(8,128)(2,1)}, u32[]{:S(2)}) copy-start(bf16[1,128,1536]{2,1,0:T(8,128)(2,1)} %param.17) | copy-start | bytes 1179652
  1042.6 627.4 %all-reduce.6.cloned.1.call-start = ((), (), s32[]{:S(2)}) async-start(), calls=%async_computation.3 | async-start | bytes 393216
  1077.7 356.5 %collective-permute-start.3 = (bf16[1,15,1536]{2,1,0:T(8,128)(2,1)S(1)}, bf16[1,15,1536]{2,1,0:T(8,128)(2,1)S(1)}, u32[]{:S(2)}, u32[]{:S(2)}) collective-permute-start(bf16[1,15,1536]{2,1,0:T(8,128)(2,1)S(1)} %get-tuple-element.366), channel_id=1, source_target_pairs={{2,0},{4,2},{6,4},{8,6},{10,8},{12,10},{14,12},{16,14},{18,16},{20... | collective-permute-start | bytes 138248 | tf_op jit(solution)/shard_map/ppermute | solution.py:20
  1082.6 351.6 %collective-permute-start.2 = (bf16[1,15,1536]{2,1,0:T(8,128)(2,1)S(1)}, bf16[1,15,1536]{2,1,0:T(8,128)(2,1)S(1)}, u32[]{:S(2)}, u32[]{:S(2)}) collective-permute-start(bf16[1,15,1536]{2,1,0:T(8,128)(2,1)S(1)} %get-tuple-element.365), channel_id=1, source_target_pairs={{0,2},{2,4},{4,6},{6,8},{8,10},{10,12},{12,14},{14,16},{16,18},{18... | collective-permute-start | bytes 138248 | tf_op jit(solution)/shard_map/ppermute | solution.py:18
  1436.5 4.7 copy-start.12
  1436.5 4.7 copy-start.17
  1436.5 4.7 copy-start.19
  1436.5 4.7 copy-start.21
  (28 other events, 117.7 us)
Sparse Core Ops, SparseCore 0:
  16.4 122.1 all-gather.5
  142.2 137.8 all-gather.7
  283.5 152.1 all-gather.3
  1042.8 31.1 all-reduce.7
  1441.3 228.7 all-reduce.5
